TPU v7x, 32 devices: a whole 2x2x4 slice. The times are simulated.
32 devices in a mesh: dp: 4 (over z), mp: 8 (over y, x, core).
Axes of the slice: x: 2, y: 2, z: 4, core: 2. Of those that a mesh axis runs over, the one named last changes fastest.
Arguments:
- accumulated: bfloat16 [4, 14336, 4096], P('dp', 'mp'), may hold values from -6 to 6
- start_q: float32 [4096, 128], replicated, may hold values from -6 to 6
Outputs:
- update: float32 [14336, 4096], P('mp')
- new_error: bfloat16 [4, 14336, 4096], P('dp', 'mp')
All inputs are finite; a program needn't handle non-finite values.
Results may differ from a plain program's by a relative error of at most 0.0059.
Values sent between devices are 32-bit elements; how exact they have to be, the bound alone decides.
A program may use at most 128 MiB of HBM per device.

v0:
```python
import jax
import jax.numpy as jnp
from jax import lax
from jax.sharding import PartitionSpec as P


def on_device(accumulated, start_q):
    corrected = accumulated[0]
    replicas = lax.axis_size("dp")
    q_bf = start_q.astype(jnp.bfloat16)
    local_p = jnp.dot(corrected, q_bf, preferred_element_type=jnp.float32)
    summed_p = lax.psum(local_p, "dp") / replicas
    gram = jnp.dot(summed_p.T, summed_p, precision=lax.Precision.HIGHEST)
    gram = lax.psum(gram, "mp")
    chol_lower = jnp.linalg.cholesky(gram)
    ortho = lax.linalg.triangular_solve(
        chol_lower, summed_p, left_side=False, lower=True, transpose_a=True
    )
    ortho_bf = ortho.astype(jnp.bfloat16)
    share = lax.psum_scatter(
        lax.dot_general(
            corrected, ortho_bf, (((0,), (0,)), ((), ())), preferred_element_type=jnp.float32
        ),
        "mp",
        scatter_dimension=0,
        tiled=True,
    )
    share = lax.psum(share, "dp")
    total_q = lax.all_gather(share, "mp", axis=0, tiled=True)
    new_q = total_q / replicas
    update = lax.dot_general(
        ortho_bf,
        new_q.astype(jnp.bfloat16),
        (((1,), (1,)), ((), ())),
        preferred_element_type=jnp.float32,
    )
    new_error = (corrected.astype(jnp.float32) - update).astype(jnp.bfloat16)
    return (update, new_error[None])


def solution(mesh):
    placed = (P("dp", "mp", None), P())
    return jax.shard_map(
        on_device,
        mesh=mesh,
        in_specs=placed,
        out_specs=(P("mp", None), P("dp", "mp", None)),
        check_vma=False,
    )
```

profile of v0, /device:TPU:0, one launch (start us, length us, event | category | flops | bytes accessed | tf_op | source)
XLA Modules:
  0.0 308.8 jit_solution(14637848607499402190)
XLA Ops:
  7.2 0.0 all-reduce.4.cloned.1.call-start
  7.2 10.7 %fusion.3 = f32[1792,128]{1,0:T(8,128)} fusion(bf16[1,1792,4096]{2,1,0:T(8,128)(2,1)} %param.2, f32[4096,128]{1,0:T(8,128)} %param.3), kind=kOutput, calls=%fused_computation.4 | convolution fusion | flops 1879572480 | bytes 17694720 | tf_op jit(solution)/shard_map/dot_general | solution.py:11
  17.9 0.0 all-reduce.4.cloned.1.call-update
  17.9 0.0 all-reduce.6.cloned.1.call-start
  18.0 50.6 %all-reduce.4.cloned.1.call-done = f32[1792,128]{1,0:T(8,128)} async-done(((f32[1792,128]{1,0:T(8,128)}), f32[1792,128]{1,0:T(8,128)}) %all-reduce.4.cloned.1.call-update) | async-done | bytes 917520 | tf_op jit(solution)/shard_map/psum | solution.py:12
  68.6 3.7 %fusion.12 = f32[128,128]{0,1:T(8,128)} fusion(f32[1792,128]{1,0:T(8,128)} %all-reduce.4.cloned.1.call-done), kind=kOutput, calls=%fused_computation.13 | convolution fusion | flops 352550912 | bytes 983040 | tf_op jit(solution)/shard_map/dot_general | solution.py:13
  72.3 0.0 all-reduce.6.cloned.1.call-update
  72.3 0.2 reduce-scatter.2.cloned.1.call-start
  72.5 52.2 %all-reduce.6.cloned.1.call-done = f32[128,128]{0,1:T(8,128)} async-done(((f32[128,128]{0,1:T(8,128)}), f32[128,128]{0,1:T(8,128)}) %all-reduce.6.cloned.1.call-update) | async-done | bytes 65552 | tf_op jit(solution)/shard_map/psum | solution.py:14
  124.8 0.9 copy.5
  125.7 0.9 fusion.18
  126.6 11.7 %cholesky.16 = f32[128,128]{1,0:T(8,128)S(1)} custom-call(f32[128,128]{1,0:T(8,128)S(1)} %fusion.18), custom_call_target="Cholesky" | custom-call | tf_op jit(solution)/shard_map/jit(cholesky)/cholesky | solution.py:15
  138.3 0.6 compare_reduce_fusion
  139.0 0.7 fusion.16
  139.6 9.8 %custom-call.6 = f32[1,128,128]{1,2,0:T(8,128)S(1)} custom-call(f32[1,128,128]{2,1,0:T(8,128)S(1)} %fusion.16), custom_call_target="InvertDiagBlocksLowerTriangular" | custom-call | tf_op jit(solution)/shard_map/triangular_solve | solution.py:16
  149.4 2.0 convolution_convert_fusion
  151.5 8.6 %fusion.5 = f32[4096,128]{0,1:T(8,128)} fusion(bf16[1792,128]{1,0:T(8,128)(2,1)S(1)} %convolution_convert_fusion, bf16[1,1792,4096]{2,1,0:T(8,128)(2,1)} %param.2), kind=kOutput, calls=%fused_computation.6 | convolution fusion | flops 1879048192 | bytes 17235968 | tf_op jit(solution)/shard_map/dot_general | solution.py:21
  160.1 0.0 reduce-scatter.2.cloned.1.call-update
  160.1 0.0 all-reduce.8.cloned.1.call-start
  160.2 40.6 %reduce-scatter.2.cloned.1.call-done = f32[512,128]{0,1:T(8,128)} async-done(((f32[4096,128]{0,1:T(8,128)}), f32[512,128]{0,1:T(8,128)}) %reduce-scatter.2.cloned.1.call-update) | async-done | bytes 262160 | tf_op jit(solution)/shard_map/reduce_scatter | solution.py:20
  200.8 0.0 all-reduce.8.cloned.1.call-update
  200.8 0.0 all-gather.2.cloned.1.call-start
  200.8 37.8 %all-reduce.8.cloned.1.call-done = f32[512,128]{0,1:T(8,128)} async-done(((f32[512,128]{0,1:T(8,128)}), f32[512,128]{0,1:T(8,128)}) %all-reduce.8.cloned.1.call-update) | async-done | bytes 262160 | tf_op jit(solution)/shard_map/psum | solution.py:28
  238.6 0.0 all-gather.2.cloned.1.call-update
  238.6 29.4 %all-gather.2.cloned.1.call-done = f32[4096,128]{0,1:T(8,128)} async-done(((f32[512,128]{0,1:T(8,128)}), f32[4096,128]{0,1:T(8,128)}) %all-gather.2.cloned.1.call-update) | async-done | bytes 2097168 | tf_op jit(solution)/shard_map/all_gather | solution.py:29
  268.0 13.9 %fusion.8 = f32[1792,4096]{1,0:T(8,128)} fusion(bf16[1792,128]{1,0:T(8,128)(2,1)S(1)} %convolution_convert_fusion, f32[4096,128]{0,1:T(8,128)} %all-gather.2.cloned.1.call-done), kind=kOutput, calls=%fused_computation.9 | convolution fusion | flops 1880096768 | bytes 31916032 | tf_op jit(solution)/shard_map/dot_general | solution.py:31
  282.0 20.3 %fusion = bf16[1,1792,4096]{2,1,0:T(8,128)(2,1)} fusion(f32[1792,4096]{1,0:T(8,128)} %fusion.8, bf16[1,1792,4096]{2,1,0:T(8,128)(2,1)} %param.2), kind=kLoop, calls=%fused_computation.1 | loop fusion | flops 22020096 | bytes 58720256 | tf_op jit(solution)/shard_map/broadcast_in_dim | solution.py:38
  (1 shorter events, 0.0 us)
Async XLA Ops:
  7.2 61.4 %all-reduce.4.cloned.1.call-start = ((), (), s32[]{:S(2)}) async-start(), calls=%async_computation.1 | async-start | bytes 1835008 | tf_op jit(solution)/shard_map/psum | solution.py:12
  17.9 106.9 %all-reduce.6.cloned.1.call-start = ((), (), s32[]{:S(2)}) async-start(), calls=%async_computation.2 | async-start | bytes 131072 | tf_op jit(solution)/shard_map/psum | solution.py:14
  72.3 128.5 %reduce-scatter.2.cloned.1.call-start = ((), (), s32[]{:S(2)}) async-start(), calls=%async_computation.3 | async-start | bytes 2359296 | tf_op jit(solution)/shard_map/reduce_scatter | solution.py:20
  160.1 78.5 %all-reduce.8.cloned.1.call-start = ((), (), s32[]{:S(2)}) async-start(), calls=%async_computation.4 | async-start | bytes 524288 | tf_op jit(solution)/shard_map/psum | solution.py:28
  200.8 67.2 %all-gather.2.cloned.1.call-start = ((), (), s32[]{:S(2)}) async-start(), calls=%async_computation.5 | async-start | bytes 2359296 | tf_op jit(solution)/shard_map/all_gather | solution.py:29
Sparse Core Ops, SparseCore 0:
  18.0 50.5 all-reduce.3
  72.4 52.2 all-reduce.5
  160.2 40.4 reduce-scatter.1
  203.0 35.5 all-reduce.7
  240.4 27.6 all-gather.1
where the time goes:
time: 309 us
  waiting for transfers between devices  211 us (68%)
  other arithmetic  44 us (14%)
  matrix products  39 us (13%)
  between operations  13.8 us (4%)
    psum x1, waiting for transfers between devices, on_device(): gram = lax.psum(gram, 'mp')  52.2 us
    psum x1, waiting for transfers between devices, on_device(): summed_p = lax.psum(local_p, 'dp') / replicas  50.6 us
    reduce_scatter x1, waiting for transfers between devices, on_device(): lax.psum_scatter(lax.dot_general(corrected, ortho_bf, (((0,), (0,)), ((),...  40.6 us
    psum x1, waiting for transfers between devices, on_device(): share = lax.psum(share, 'dp')  37.8 us
    all_gather x1, waiting for transfers between devices, on_device(): total_q = lax.all_gather(share, 'mp', axis=0, tiled=True)  29.4 us
    broadcast_in_dim x1, other arithmetic, on_device(): return (update, new_error[None])  20.3 us
    dot_general x1, matrix products, on_device(): lax.dot_general(ortho_bf, new_q.astype(jnp.bfloat16), (((1,), (1,)), ((),...  13.9 us
    another operation x3, other arithmetic, on_device(): chol_lower = jnp.linalg.cholesky(gram)  12.4 us
  transfers between devices with their start and end apart: 5, of which 5 were waited for; matrix products, arithmetic and copies ran while one was open for 0% of the time, Pallas kernels for 0%

commit v1 on v0

v1 whole, which is shorter than its diff:
```python
import functools

import jax
import jax.numpy as jnp
from jax import lax
from jax.experimental import pallas as pl
from jax.experimental.pallas import tpu as pltpu
from jax.sharding import PartitionSpec as P

MESH = pl.DeviceIdType.MESH
HIGHEST = lax.Precision.HIGHEST
VMEM_BYTES = 60 * 1024 * 1024


def chunks_of(rows):
    for count in (14, 7, 8, 4, 2):
        if rows % (16 * count) == 0:
            return count
    return 1


def copy_to(axis, target, src, dst, send_sem, recv_sem):
    return pltpu.make_async_remote_copy(
        src_ref=src, dst_ref=dst, send_sem=send_sem, recv_sem=recv_sem,
        device_id={axis: target}, device_id_type=MESH,
    )


def greet_line(barrier, n, d):
    @pl.when(d > 0)
    def _():
        pl.semaphore_signal(barrier, inc=1, device_id={"dp": d - 1}, device_id_type=MESH)

    @pl.when(d < n - 1)
    def _():
        pl.semaphore_signal(barrier, inc=1, device_id={"dp": d + 1}, device_id_type=MESH)


def line_of(n, d):
    half = n // 2
    left = d < half
    inner = jnp.where(left, d + 1, d - 1)
    outer = jnp.where(left, d - 1, d + 1)
    edge = (d == 0) | (d == n - 1)
    mid = (d == half - 1) | (d == half)
    return inner, outer, edge, mid


def left_kernel(n, count, a_hbm, q_ref, s_ref, zt_ref, gram_ref, a_v, own, part, cross, tot, acc,
                a_sem, in_send, out_send, part_recv, cross_recv, tot_recv):
    rows, wide = a_hbm.shape
    rank = q_ref.shape[1]
    rb = rows // count
    d = lax.axis_index("dp")
    inner, outer, edge, mid = line_of(n, d)

    def at(c):
        return pl.ds(pl.multiple_of(c * rb, rb), rb)

    def load(c):
        return pltpu.make_async_copy(a_hbm.at[at(c)], a_v.at[at(c)], a_sem.at[c])

    def send_part(c):
        return copy_to("dp", inner, own.at[at(c)], part.at[at(c)], in_send.at[c], part_recv.at[c])

    def send_cross(c):
        return copy_to("dp", inner, own.at[at(c)], cross.at[at(c)], in_send.at[c], cross_recv.at[c])

    def send_tot(c):
        return copy_to("dp", outer, tot.at[at(c)], tot.at[at(c)], out_send.at[c], tot_recv.at[c])

    def send_inward(c):
        @pl.when(mid)
        def _():
            send_cross(c).start()

        @pl.when(jnp.logical_not(mid))
        def _():
            send_part(c).start()

    for c in range(count):
        load(c).start()
    barrier = pltpu.get_barrier_semaphore()
    greet_line(barrier, n, d)
    q_bf = q_ref[...].astype(jnp.bfloat16)
    acc[...] = jnp.zeros_like(acc)
    gram_ref[...] = jnp.zeros_like(gram_ref)
    pl.semaphore_wait(barrier, jnp.where(d > 0, 1, 0) + jnp.where(d < n - 1, 1, 0))

    def multiply(c, carry):
        load(c).wait()
        own[at(c), :] = jnp.dot(a_v[at(c), :], q_bf, preferred_element_type=jnp.float32)

        @pl.when(edge)
        def _():
            send_inward(c)

        return carry

    lax.fori_loop(0, count, multiply, 0)
    lag = 1

    def exchange(t, carry):
        @pl.when(jnp.logical_not(edge) & (t < count))
        def _():
            send_part(t).wait_recv()
            own[at(t), :] = own[at(t), :] + part[at(t), :]
            send_inward(t)

        @pl.when(t >= lag)
        def _():
            c = t - lag

            @pl.when(mid)
            def _():
                send_cross(c).wait_recv()
                tot[at(c), :] = own[at(c), :] + cross[at(c), :]

            @pl.when(jnp.logical_not(mid))
            def _():
                send_tot(c).wait_recv()

            @pl.when(jnp.logical_not(edge))
            def _():
                send_tot(c).start()

            mean = tot[at(c), :] / n
            s_ref[at(c), :] = mean
            turned = mean.T
            gram_ref[...] += jnp.dot(turned, mean, precision=HIGHEST, preferred_element_type=jnp.float32)
            high = turned.astype(jnp.bfloat16)
            low = (turned - high.astype(jnp.float32)).astype(jnp.bfloat16)
            both = jnp.concatenate([high, low], axis=0)
            step = 512
            for col in range(0, wide, step):
                acc[:, col:col + step] += jnp.dot(
                    both, a_v[at(c), col:col + step], preferred_element_type=jnp.float32
                )

        return carry

    lax.fori_loop(0, count + lag, exchange, 0)
    for block in range(wide // 128):
        cols = slice(block * 128, block * 128 + 128)
        zt_ref[block * rank:(block + 1) * rank, :] = acc[:rank, cols] + acc[rank:, cols]

    def drain(c, carry):
        send_part(c).wait_send()

        @pl.when(jnp.logical_not(edge))
        def _():
            send_tot(c).wait_send()

        return carry

    lax.fori_loop(0, count, drain, 0)


def eliminate(m_ref, first, last):
    size = m_ref.shape[0]
    row = lax.broadcasted_iota(jnp.int32, (size, size), 0)
    lane = lax.broadcasted_iota(jnp.int32, (size, size), 1)

    def pivot(k, carry):
        m = m_ref[...]
        here = lane == k
        col = jnp.sum(jnp.where(here, m, 0.0), axis=1, keepdims=True)
        line = m_ref[pl.ds(k, 1), :]
        lane1 = lax.broadcasted_iota(jnp.int32, line.shape, 1)
        value = jnp.sum(jnp.where(lane1 == k, line, 0.0), axis=1, keepdims=True)
        below = row > k
        factor = col * (1.0 / value)
        line = jnp.where(lane1 == k, 1.0, line)
        m_ref[...] = jnp.where(below, jnp.where(here, 0.0, m) - factor * line, m)
        return carry

    lax.fori_loop(first, last, pivot, 0)


def right_kernel(n, bits, zt_ref, gram_ref, nq_ref, w_ref, z, got, full, gwork, ggot, m_ref,
                 part, cross, rs_send, rs_recv, ag_send, ag_recv, g_send, g_recv,
                 in_send, out_send, part_recv, cross_recv, tot_recv):
    wide, rank = zt_ref.shape
    d = lax.axis_index("dp")
    me = lax.axis_index("mp")
    inner, outer, edge, mid = line_of(n, d)

    def bit(b):
        return lax.rem(me // (1 << b), 2)

    def partner(b):
        return me + (1 - 2 * bit(b)) * (1 << b)

    barrier = pltpu.get_barrier_semaphore()
    greet_line(barrier, n, d)
    for b in range(bits):
        pl.semaphore_signal(barrier, inc=1, device_id={"mp": partner(b)}, device_id_type=MESH)
    pl.semaphore_wait(barrier, jnp.where(d > 0, 1, 0) + jnp.where(d < n - 1, 1, 0) + bits)

    orders = (tuple(range(bits)), (0,) + tuple(range(bits - 1, 0, -1)))
    length = wide // 2
    offs = [0, length]
    gwork[0] = gram_ref[...]
    spot = 0
    for j in range(bits):
        half = length // 2
        source = zt_ref if j == 0 else z
        copies, keeps = [], []
        for s in range(2):
            b = orders[s][j]
            keeps.append(pl.multiple_of(offs[s] + bit(b) * half, half))
            away = pl.multiple_of(offs[s] + (1 - bit(b)) * half, half)
            copies.append(copy_to(
                "mp", partner(b), source.at[pl.ds(away, half)], got.at[s, pl.ds(spot, half)],
                rs_send.at[s, j], rs_recv.at[s, j],
            ))
        gcopy = copy_to("mp", partner(j), gwork.at[j], ggot.at[j], g_send.at[j], g_recv.at[j])
        gcopy.start()
        for copy in copies:
            copy.start()
        gcopy.wait()
        gwork[j + 1] = gwork[j] + ggot[j]
        for s in range(2):
            copies[s].wait()
            z[pl.ds(keeps[s], half), :] = source[pl.ds(keeps[s], half), :] + got[s, spot:spot + half, :]
        offs = keeps
        spot += half
        length = half
    m_ref[...] = gwork[bits]

    def own(s):
        return z.at[pl.ds(offs[s], length)]

    def tot(s):
        return full.at[pl.ds(offs[s], length)]

    def send_part(s):
        return copy_to("dp", inner, own(s), part.at[s], in_send.at[s], part_recv.at[s])

    def send_cross(s):
        return copy_to("dp", inner, own(s), cross.at[s], in_send.at[s], cross_recv.at[s])

    def send_tot(s):
        return copy_to("dp", outer, tot(s), tot(s), out_send.at[s], tot_recv.at[s])

    def send_inward(s):
        @pl.when(mid)
        def _():
            send_cross(s).start()

        @pl.when(jnp.logical_not(mid))
        def _():
            send_part(s).start()

    for s in range(2):
        @pl.when(jnp.logical_not(edge))
        def _():
            send_part(s).wait_recv()
            own(s)[...] = own(s)[...] + part[s]

        send_inward(s)
    for s in range(2):
        @pl.when(mid)
        def _():
            send_cross(s).wait_recv()
            tot(s)[...] = own(s)[...] + cross[s]

        @pl.when(jnp.logical_not(mid))
        def _():
            send_tot(s).wait_recv()

        @pl.when(jnp.logical_not(edge))
        def _():
            send_tot(s).start()

    done = 0
    for j in range(bits - 1, -1, -1):
        copies = []
        for s in range(2):
            b = orders[s][j]
            mine = full.at[pl.ds(offs[s], length)]
            copies.append(copy_to("mp", partner(b), mine, mine, ag_send.at[s, j], ag_recv.at[s, j]))
        for copy in copies:
            copy.start()
        upto = rank if j == 0 else done + rank // bits
        eliminate(m_ref, done, upto)
        done = upto
        for s in range(2):
            copies[s].wait()
            offs[s] = pl.multiple_of(offs[s] - bit(orders[s][j]) * length, length)
        length *= 2

    m = m_ref[...]
    row = lax.broadcasted_iota(jnp.int32, (rank, rank), 0)
    lane = lax.broadcasted_iota(jnp.int32, (rank, rank), 1)
    pivots = jnp.sum(jnp.where(row == lane, m, 0.0), axis=1, keepdims=True)
    w = jnp.where(lane < row, m, jnp.where(lane == row, 1.0, 0.0)) / jnp.sqrt(pivots)
    w_ref[...] = w

    def turn(block, carry):
        rows = pl.ds(pl.multiple_of(block * rank, rank), rank)
        nq_ref[rows, :] = (
            jnp.dot(w, full[rows, :], precision=HIGHEST, preferred_element_type=jnp.float32) / n
        ).astype(jnp.bfloat16)
        return carry

    lax.fori_loop(0, wide // rank, turn, 0)
    for s in range(2):
        copy_to("dp", inner, part.at[s], part.at[s], in_send.at[s], part_recv.at[s]).wait_send()

        @pl.when(jnp.logical_not(edge))
        def _():
            copy_to("dp", outer, part.at[s], part.at[s], out_send.at[s], tot_recv.at[s]).wait_send()


def last_kernel(a_ref, s_ref, w_ref, nq_ref, update_ref, error_ref):
    rank = w_ref.shape[0]
    ortho = lax.dot_general(
        s_ref[...], w_ref[...], (((1,), (1,)), ((), ())), precision=HIGHEST,
        preferred_element_type=jnp.float32,
    ).astype(jnp.bfloat16)
    group = 4
    for first in range(0, nq_ref.shape[0] // rank, group):
        right = jnp.concatenate(
            [nq_ref[b * rank:(b + 1) * rank, :] for b in range(first, first + group)], axis=1
        )
        cols = slice(first * 128, (first + group) * 128)
        update = jnp.dot(ortho, right, preferred_element_type=jnp.float32)
        update_ref[:, cols] = update
        error_ref[:, cols] = (a_ref[:, cols].astype(jnp.float32) - update).astype(jnp.bfloat16)


def on_device(accumulated, start_q):
    a = accumulated[0]
    rows, wide = a.shape
    rank = start_q.shape[1]
    n, peers = lax.axis_size("dp"), lax.axis_size("mp")
    bits = peers.bit_length() - 1
    assert peers == 1 << bits and n >= 2 and rank == 128
    count = chunks_of(rows)
    f32, bf16 = jnp.float32, jnp.bfloat16
    vmem = pl.BlockSpec(memory_space=pltpu.VMEM)
    dma = pltpu.SemaphoreType.DMA
    summed, zt, gram = pl.pallas_call(
        functools.partial(left_kernel, n, count),
        out_shape=(
            jax.ShapeDtypeStruct((rows, rank), f32),
            jax.ShapeDtypeStruct((wide // 128 * rank, 128), f32),
            jax.ShapeDtypeStruct((rank, rank), f32),
        ),
        in_specs=[pl.BlockSpec(memory_space=pl.ANY), vmem],
        out_specs=(vmem, vmem, vmem),
        scratch_shapes=[
            pltpu.VMEM((rows, wide), bf16),
            pltpu.VMEM((rows, rank), f32),
            pltpu.VMEM((rows, rank), f32),
            pltpu.VMEM((rows, rank), f32),
            pltpu.VMEM((rows, rank), f32),
            pltpu.VMEM((2 * rank, wide), f32),
        ] + [dma((count,))] * 6,
        compiler_params=pltpu.CompilerParams(
            collective_id=0, has_side_effects=True, vmem_limit_bytes=VMEM_BYTES
        ),
        name="left_factor",
    )(a, start_q)
    share = wide // 2 // peers
    new_q, w = pl.pallas_call(
        functools.partial(right_kernel, n, bits),
        out_shape=(
            jax.ShapeDtypeStruct((wide, rank), bf16),
            jax.ShapeDtypeStruct((rank, rank), f32),
        ),
        in_specs=[vmem, vmem],
        out_specs=(vmem, vmem),
        scratch_shapes=[
            pltpu.VMEM((wide, rank), f32),
            pltpu.VMEM((2, wide // 2, rank), f32),
            pltpu.VMEM((wide, rank), f32),
            pltpu.VMEM((bits + 1, rank, rank), f32),
            pltpu.VMEM((bits, rank, rank), f32),
            pltpu.VMEM((rank, rank), f32),
            pltpu.VMEM((2, share, rank), f32),
            pltpu.VMEM((2, share, rank), f32),
        ] + [dma((2, bits))] * 4 + [dma((bits,))] * 2 + [dma((2,))] * 5,
        compiler_params=pltpu.CompilerParams(
            collective_id=1, has_side_effects=True, vmem_limit_bytes=VMEM_BYTES
        ),
        name="right_factor",
    )(zt, gram)
    rb = rows // count
    update, error = pl.pallas_call(
        last_kernel,
        grid=(count,),
        out_shape=(
            jax.ShapeDtypeStruct((rows, wide), f32),
            jax.ShapeDtypeStruct((rows, wide), bf16),
        ),
        in_specs=[
            pl.BlockSpec((rb, wide), lambda i: (i, 0)),
            pl.BlockSpec((rb, rank), lambda i: (i, 0)),
            pl.BlockSpec((rank, rank), lambda i: (0, 0)),
            pl.BlockSpec((wide, rank), lambda i: (0, 0)),
        ],
        out_specs=(
            pl.BlockSpec((rb, wide), lambda i: (i, 0)),
            pl.BlockSpec((rb, wide), lambda i: (i, 0)),
        ),
        name="decompress",
    )(a, summed, w, new_q)
    return (update, error[None])


def solution(mesh):
    placed = (P("dp", "mp", None), P())
    return jax.shard_map(
        on_device,
        mesh=mesh,
        in_specs=placed,
        out_specs=(P("mp", None), P("dp", "mp", None)),
        check_vma=False,
    )
```

time: 309 us -> 132 us (0.43)
  waiting for transfers between devices: 211 us -> 0 us
  Pallas kernels: 0 us -> 131 us
  other arithmetic: 44 us -> 0 us
  matrix products: 39 us -> 0 us
  between operations: 13.8 us -> 0.65 us
    psum x3 -> x0, waiting for transfers between devices: 141 us -> none  [the longest x1 52.2 us: on_device(): gram = lax.psum(gram, 'mp')]
    pallas_call x0 -> x3, Pallas kernels: none -> 131 us  [the longest x1 58.2 us: on_device(): pl.pallas_call(functools.partial(right_kernel, n, bits), out_shape=(jax.S...]
    reduce_scatter x1 -> x0, waiting for transfers between devices: 40.6 us -> none  [on_device(): lax.psum_scatter(lax.dot_general(corrected, ortho_bf, (((0,), (0,)), ((),...]
    dot_general x4 -> x0, matrix products: 36.9 us -> none  [the longest x1 13.9 us: on_device(): lax.dot_general(ortho_bf, new_q.astype(jnp.bfloat16), (((1,), (1,)), ((),...]
    all_gather x1 -> x0, waiting for transfers between devices: 29.4 us -> none  [on_device(): total_q = lax.all_gather(share, 'mp', axis=0, tiled=True)]
    another operation x5 -> x0, other arithmetic: 22.9 us -> none  [the longest x3 12.4 us: on_device(): chol_lower = jnp.linalg.cholesky(gram)]
    broadcast_in_dim x1 -> x0, other arithmetic: 20.3 us -> none  [on_device(): return (update, new_error[None])]
  transfers between devices with their start and end apart: 5 -> 0, of which waited for: 5 -> 0; matrix products, arithmetic and copies ran while one was open for 0% -> 0% of each run, Pallas kernels for 0% -> 0%
where the time goes in v1:
time: 132 us
  Pallas kernels  131 us (99%)
    pallas_call x1, Pallas kernels, on_device(): pl.pallas_call(functools.partial(right_kernel, n, bits), out_shape=(jax.S...  58.2 us
    pallas_call x1, Pallas kernels, on_device(): pl.pallas_call(functools.partial(left_kernel, n, count), out_shape=(jax.S...  49.2 us
    pallas_call x1, Pallas kernels, on_device(): pl.pallas_call(last_kernel, grid=(count,), out_shape=(jax.ShapeDtypeStruc...  23.6 us

profile of v1, /device:TPU:0, one launch (start us, length us, event | category | flops | bytes accessed | tf_op | source)
XLA Modules:
  0.0 131.7 jit_solution(16150059178156541916)
XLA Ops:
  0.6 49.2 %left_factor.1 = (f32[1792,128]{1,0:T(8,128)}, f32[4096,128]{1,0:T(8,128)}, f32[128,128]{1,0:T(8,128)}) custom-call(bf16[1792,4096]{1,0:T(8,128)(2,1)} %bitcast.2, f32[4096,128]{1,0:T(8,128)} %q_ref.1), custom_call_target="tpu_custom_call" | custom-call | tf_op jit(solution)/shard_map/left_factor/pallas_call | solution.py:344
  49.8 58.2 %right_factor.1 = (bf16[4096,128]{1,0:T(8,128)(2,1)}, f32[128,128]{1,0:T(8,128)}) custom-call(f32[4096,128]{1,0:T(8,128)} %get-tuple-element.10.zt_ref, f32[128,128]{1,0:T(8,128)} %get-tuple-element.11.gram_ref), custom_call_target="tpu_custom_call" | custom-call | tf_op jit(solution)/shard_map/right_factor/pallas_call | solution.py:367
  108.0 23.6 %decompress.1 = (f32[1792,4096]{1,0:T(8,128)}, bf16[1792,4096]{1,0:T(8,128)(2,1)}) custom-call(bf16[1792,4096]{1,0:T(8,128)(2,1)} %bitcast.3, f32[1792,128]{1,0:T(8,128)} %get-tuple-element.9.s_ref, f32[128,128]{1,0:T(8,128)} %get-tuple-element.12.w_ref, bf16[4096,128]{1,0:T(8,128)(2,1)} %get-tuple-element.13.nq_ref), custom_call_target="tpu_custom_call" | custom-call | tf_op jit(solution)/shard_map/decompress/pallas_call | solution.py:391

commit v2 on v0

v2 whole, which is shorter than its diff:
```python
import functools

import jax
import jax.numpy as jnp
from jax import lax
from jax.experimental import pallas as pl
from jax.experimental.pallas import tpu as pltpu
from jax.sharding import PartitionSpec as P

MESH = pl.DeviceIdType.MESH
HIGHEST = lax.Precision.HIGHEST
GROUPS = 2
VMEM_BYTES = 60 * 1024 * 1024


def chunks_of(rows):
    for count in (7, 8, 14, 4, 2):
        if rows % (128 * count) == 0:
            return count
    return 1


def copy_to(axis, target, src, dst, send_sem, recv_sem):
    return pltpu.make_async_remote_copy(
        src_ref=src, dst_ref=dst, send_sem=send_sem, recv_sem=recv_sem,
        device_id={axis: target}, device_id_type=MESH,
    )


def greet_line(barrier, n, d):
    @pl.when(d > 0)
    def _():
        pl.semaphore_signal(barrier, inc=1, device_id={"dp": d - 1}, device_id_type=MESH)

    @pl.when(d < n - 1)
    def _():
        pl.semaphore_signal(barrier, inc=1, device_id={"dp": d + 1}, device_id_type=MESH)


def line_of(n, d):
    half = n // 2
    left = d < half
    inner = jnp.where(left, d + 1, d - 1)
    outer = jnp.where(left, d - 1, d + 1)
    edge = (d == 0) | (d == n - 1)
    mid = (d == half - 1) | (d == half)
    return inner, outer, edge, mid


def factors_kernel(n, bits, count, a_hbm, q_ref, s_ref, nq_ref, w_ref, a_v, own, part, cross, acc, z, got,
                   full, gwork, ggot, m_ref, zpart, zcross, a_sem, in_send, out_send, part_recv, cross_recv,
                   tot_recv, rs_send, rs_recv, ag_send, ag_recv, g_send, g_recv, zin_send, zout_send,
                   zpart_recv, zcross_recv, ztot_recv):
    rows, wide = a_hbm.shape
    rank = q_ref.shape[1]
    rg = rank // GROUPS
    rb = rows // count
    blocks = wide // 128
    d = lax.axis_index("dp")
    me = lax.axis_index("mp")
    inner, outer, edge, mid = line_of(n, d)
    tot = s_ref

    def bit(b):
        return lax.rem(me // (1 << b), 2)

    def partner(b):
        return me + (1 - 2 * bit(b)) * (1 << b)

    def load(c):
        some = pl.ds(pl.multiple_of(c * rb, rb), rb)
        return pltpu.make_async_copy(a_hbm.at[some], a_v.at[some], a_sem.at[c])

    def piece(ref, g, c):
        return ref.at[c, g * rg:(g + 1) * rg]

    def send_part(g, c):
        return copy_to("dp", inner, piece(own, g, c), piece(part, g, c), in_send.at[g, c], part_recv.at[g, c])

    def send_cross(g, c):
        return copy_to("dp", inner, piece(own, g, c), piece(cross, g, c), in_send.at[g, c], cross_recv.at[g, c])

    def send_tot(g, c):
        return copy_to("dp", outer, piece(tot, g, c), piece(tot, g, c), out_send.at[g, c], tot_recv.at[g, c])

    def inward(crossing, passing):
        @pl.when(mid)
        def _():
            crossing.start()

        @pl.when(jnp.logical_not(mid))
        def _():
            passing.start()

    for c in range(count):
        load(c).start()
    barrier = pltpu.get_barrier_semaphore()
    greet_line(barrier, n, d)
    for b in range(bits):
        pl.semaphore_signal(barrier, inc=1, device_id={"mp": partner(b)}, device_id_type=MESH)
    q_bf = q_ref[...].astype(jnp.bfloat16)
    gwork[0] = jnp.zeros_like(gwork[0])
    pl.semaphore_wait(barrier, jnp.where(d > 0, 1, 0) + jnp.where(d < n - 1, 1, 0) + bits)

    def multiply(c, carry):
        load(c).wait()
        some = pl.ds(pl.multiple_of(c * rb, rb), rb)
        own[c] = jnp.dot(a_v[some, :], q_bf, preferred_element_type=jnp.float32).T

        @pl.when(edge)
        def _():
            inward(send_cross(0, c), send_part(0, c))

        return carry

    lax.fori_loop(0, count, multiply, 0)

    @pl.when(edge)
    def _():
        for c in range(count):
            inward(send_cross(1, c), send_part(1, c))

    lag = 1

    def exchange(g, t, carry):
        @pl.when(jnp.logical_not(edge) & (t < count))
        def _():
            send_part(g, t).wait_recv()
            mine = piece(own, g, t)
            mine[...] = mine[...] + piece(part, g, t)[...]
            inward(send_cross(g, t), send_part(g, t))

        @pl.when(t >= lag)
        def _():
            c = t - lag

            @pl.when(mid)
            def _():
                send_cross(g, c).wait_recv()
                piece(tot, g, c)[...] = piece(own, g, c)[...] + piece(cross, g, c)[...]

            @pl.when(jnp.logical_not(mid))
            def _():
                send_tot(g, c).wait_recv()

            @pl.when(jnp.logical_not(edge))
            def _():
                send_tot(g, c).start()

            mean = piece(tot, g, c)[...] / n
            high = mean.astype(jnp.bfloat16)
            low = (mean - high.astype(jnp.float32)).astype(jnp.bfloat16)
            both = jnp.concatenate([high, low], axis=0)
            some = pl.ds(pl.multiple_of(c * rb, rb), rb)
            step = 512
            for col in range(0, wide, step):
                acc[g, :, col:col + step] += jnp.dot(
                    both, a_v[some, col:col + step], preferred_element_type=jnp.float32
                )
            if g == GROUPS - 1:
                whole = tot[c] / n
                gwork[0] += lax.dot_general(
                    whole, whole, (((1,), (1,)), ((), ())), precision=HIGHEST,
                    preferred_element_type=jnp.float32,
                )

        return carry

    def run(g, first, last):
        lax.fori_loop(first, last, functools.partial(exchange, g), 0)

    def build(g):
        for block in range(blocks):
            cols = slice(block * 128, block * 128 + 128)
            z[g, block * rg:(block + 1) * rg, :] = acc[g, :rg, cols] + acc[g, rg:, cols]

    orders = (tuple(range(bits)), (0,) + tuple(range(bits - 1, 0, -1)))
    lengths = [blocks * rg // 2 >> j for j in range(bits + 1)]
    offs = []
    for s in range(2):
        at = [s * lengths[0]]
        for j in range(bits):
            at.append(pl.multiple_of(at[j] + bit(orders[s][j]) * lengths[j + 1], lengths[bits]))
        offs.append(at)

    def rs(g, s, j):
        half = lengths[j + 1]
        b = orders[s][j]
        away = pl.multiple_of(offs[s][j] + (1 - bit(b)) * half, lengths[bits])
        spot = lengths[0] - lengths[j]
        return copy_to(
            "mp", partner(b), z.at[g, pl.ds(away, half)], got.at[g, s, spot:spot + half],
            rs_send.at[g, s, j], rs_recv.at[g, s, j],
        )

    def rs_start(g, j):
        for s in range(2):
            rs(g, s, j).start()

    def rs_finish(g, j):
        half, spot = lengths[j + 1], lengths[0] - lengths[j]
        for s in range(2):
            rs(g, s, j).wait()
            keep = pl.ds(offs[s][j + 1], half)
            z[g, keep, :] = z[g, keep, :] + got[g, s, spot:spot + half, :]

    def gram(j):
        return copy_to("mp", partner(j), gwork.at[j], ggot.at[j], g_send.at[j], g_recv.at[j])

    def gram_finish(j):
        gram(j).wait()
        gwork[j + 1] = gwork[j] + ggot[j]

    def share(ref, g, s):
        return ref.at[g, pl.ds(offs[s][bits], lengths[bits])]

    def z_part(g, s):
        return copy_to("dp", inner, share(z, g, s), zpart.at[g, s], zin_send.at[g, s], zpart_recv.at[g, s])

    def z_cross(g, s):
        return copy_to("dp", inner, share(z, g, s), zcross.at[g, s], zin_send.at[g, s], zcross_recv.at[g, s])

    def z_tot(g, s):
        return copy_to("dp", outer, share(full, g, s), share(full, g, s), zout_send.at[g, s], ztot_recv.at[g, s])

    def line_edge(g):
        @pl.when(edge)
        def _():
            for s in range(2):
                inward(z_cross(g, s), z_part(g, s))

    def line_in(g):
        @pl.when(jnp.logical_not(edge))
        def _():
            for s in range(2):
                z_part(g, s).wait_recv()
                mine = share(z, g, s)
                mine[...] = mine[...] + zpart[g, s]
                inward(z_cross(g, s), z_part(g, s))

    def line_out(g):
        for s in range(2):
            @pl.when(mid)
            def _():
                z_cross(g, s).wait_recv()
                share(full, g, s)[...] = share(z, g, s)[...] + zcross[g, s]

            @pl.when(jnp.logical_not(mid))
            def _():
                z_tot(g, s).wait_recv()

            @pl.when(jnp.logical_not(edge))
            def _():
                z_tot(g, s).start()

    def ag(g, s, j):
        mine = full.at[g, pl.ds(offs[s][j + 1], lengths[j + 1])]
        return copy_to("mp", partner(orders[s][j]), mine, mine, ag_send.at[g, s, j], ag_recv.at[g, s, j])

    def ag_start(g, j):
        for s in range(2):
            ag(g, s, j).start()

    def ag_finish(g, j):
        for s in range(2):
            ag(g, s, j).wait()

    acc[...] = jnp.zeros_like(acc)
    run(0, 0, count + lag)
    build(0)
    rs_start(0, 0)
    steps = count + lag
    at = 0
    for j in range(bits):
        upto = steps * (j + 1) // bits
        run(1, at, upto)
        at = upto
        if j < bits - 1:
            rs_finish(0, j)
            rs_start(0, j + 1)
    gram(0).start()
    build(1)
    rs_start(1, 0)
    rs_finish(0, bits - 1)
    line_edge(0)
    for j in range(bits):
        gram_finish(j)
        if j < bits - 1:
            gram(j + 1).start()
        if j == 1:
            line_out(0)
            ag_start(0, bits - 1)
        rs_finish(1, j)
        if j < bits - 1:
            rs_start(1, j + 1)
        if j == 0:
            line_in(0)
    line_edge(1)
    m_ref[...] = gwork[bits]
    portion = rank // 8
    eliminate(m_ref, 0, portion)
    line_in(1)
    ag_finish(0, bits - 1)
    ag_start(0, bits - 2)
    eliminate(m_ref, portion, 2 * portion)
    line_out(1)
    ag_start(1, bits - 1)
    done = 2 * portion
    for j in range(bits - 2, -1, -1):
        upto = rank if j == 0 else done + (rank - done) // (bits - 1)
        eliminate(m_ref, done, upto)
        done = upto
        ag_finish(0, j)
        if j > 0:
            ag_start(0, j - 1)
        ag_finish(1, j + 1)
        ag_start(1, j)

    m = m_ref[...]
    row = lax.broadcasted_iota(jnp.int32, (rank, rank), 0)
    lane = lax.broadcasted_iota(jnp.int32, (rank, rank), 1)
    pivots = jnp.sum(jnp.where(row == lane, m, 0.0), axis=1, keepdims=True)
    w = jnp.where(lane < row, m, jnp.where(lane == row, 1.0, 0.0)) / jnp.sqrt(pivots)
    w_ref[...] = w
    ag_finish(1, 0)

    def turn(block, carry):
        rows_of = pl.ds(pl.multiple_of(block * rg, rg), rg)
        right = jnp.concatenate([full[g, rows_of, :] for g in range(GROUPS)], axis=0)
        nq_ref[pl.ds(pl.multiple_of(block * rank, rank), rank), :] = (
            jnp.dot(w, right, precision=HIGHEST, preferred_element_type=jnp.float32) / n
        ).astype(jnp.bfloat16)
        return carry

    lax.fori_loop(0, blocks, turn, 0)
    for g in range(GROUPS):
        for c in range(count):
            send_part(g, c).wait_send()
        for s in range(2):
            z_part(g, s).wait_send()

        @pl.when(jnp.logical_not(edge))
        def _():
            for c in range(count):
                send_tot(g, c).wait_send()
            for s in range(2):
                z_tot(g, s).wait_send()


def eliminate(m_ref, first, last):
    size = m_ref.shape[0]
    row = lax.broadcasted_iota(jnp.int32, (size, size), 0)
    lane = lax.broadcasted_iota(jnp.int32, (size, size), 1)

    def pivot(k, carry):
        m = m_ref[...]
        here = lane == k
        col = jnp.sum(jnp.where(here, m, 0.0), axis=1, keepdims=True)
        line = m_ref[pl.ds(k, 1), :]
        lane1 = lax.broadcasted_iota(jnp.int32, line.shape, 1)
        value = jnp.sum(jnp.where(lane1 == k, line, 0.0), axis=1, keepdims=True)
        below = row > k
        factor = col * (1.0 / value)
        line = jnp.where(lane1 == k, 1.0, line)
        m_ref[...] = jnp.where(below, jnp.where(here, 0.0, m) - factor * line, m)
        return carry

    lax.fori_loop(first, last, pivot, 0)


def last_kernel(n, a_ref, s_ref, w_ref, nq_ref, update_ref, error_ref):
    rank = w_ref.shape[0]
    ortho = jnp.dot(
        w_ref[...], s_ref[0] / n, precision=HIGHEST, preferred_element_type=jnp.float32
    ).T.astype(jnp.bfloat16)
    group = 4
    for first in range(0, nq_ref.shape[0] // rank, group):
        right = jnp.concatenate(
            [nq_ref[b * rank:(b + 1) * rank, :] for b in range(first, first + group)], axis=1
        )
        cols = slice(first * 128, (first + group) * 128)
        update = jnp.dot(ortho, right, preferred_element_type=jnp.float32)
        update_ref[:, cols] = update
        error_ref[:, cols] = (a_ref[:, cols].astype(jnp.float32) - update).astype(jnp.bfloat16)


def on_device(accumulated, start_q):
    a = accumulated[0]
    rows, wide = a.shape
    rank = start_q.shape[1]
    n, peers = lax.axis_size("dp"), lax.axis_size("mp")
    bits = peers.bit_length() - 1
    assert peers == 1 << bits and bits >= 2 and n >= 2 and rank == 128
    count = chunks_of(rows)
    rb = rows // count
    f32, bf16 = jnp.float32, jnp.bfloat16
    vmem = pl.BlockSpec(memory_space=pltpu.VMEM)
    dma = pltpu.SemaphoreType.DMA
    flat = wide // GROUPS
    summed, new_q, w = pl.pallas_call(
        functools.partial(factors_kernel, n, bits, count),
        out_shape=(
            jax.ShapeDtypeStruct((count, rank, rb), f32),
            jax.ShapeDtypeStruct((wide, rank), bf16),
            jax.ShapeDtypeStruct((rank, rank), f32),
        ),
        in_specs=[pl.BlockSpec(memory_space=pl.ANY), vmem],
        out_specs=(vmem, vmem, vmem),
        scratch_shapes=[
            pltpu.VMEM((rows, wide), bf16),
            pltpu.VMEM((count, rank, rb), f32),
            pltpu.VMEM((count, rank, rb), f32),
            pltpu.VMEM((count, rank, rb), f32),
            pltpu.VMEM((GROUPS, 2 * rank // GROUPS, wide), f32),
            pltpu.VMEM((GROUPS, flat, 128), f32),
            pltpu.VMEM((GROUPS, 2, flat // 2, 128), f32),
            pltpu.VMEM((GROUPS, flat, 128), f32),
            pltpu.VMEM((bits + 1, rank, rank), f32),
            pltpu.VMEM((bits, rank, rank), f32),
            pltpu.VMEM((rank, rank), f32),
            pltpu.VMEM((GROUPS, 2, flat // 2 // peers, 128), f32),
            pltpu.VMEM((GROUPS, 2, flat // 2 // peers, 128), f32),
            dma((count,)),
        ] + [dma((GROUPS, count))] * 5 + [dma((GROUPS, 2, bits))] * 4 + [dma((bits,))] * 2
        + [dma((GROUPS, 2))] * 5,
        compiler_params=pltpu.CompilerParams(
            collective_id=0, has_side_effects=True, vmem_limit_bytes=VMEM_BYTES
        ),
        name="factors",
    )(a, start_q)
    split = 2 if rb % 256 == 0 else 1
    small = rb // split
    update, error = pl.pallas_call(
        functools.partial(last_kernel, n),
        grid=(count, split),
        out_shape=(
            jax.ShapeDtypeStruct((rows, wide), f32),
            jax.ShapeDtypeStruct((rows, wide), bf16),
        ),
        in_specs=[
            pl.BlockSpec((small, wide), lambda i, j: (i * split + j, 0)),
            pl.BlockSpec((1, rank, small), lambda i, j: (i, 0, j)),
            pl.BlockSpec((rank, rank), lambda i, j: (0, 0)),
            pl.BlockSpec((wide, rank), lambda i, j: (0, 0)),
        ],
        out_specs=(
            pl.BlockSpec((small, wide), lambda i, j: (i * split + j, 0)),
            pl.BlockSpec((small, wide), lambda i, j: (i * split + j, 0)),
        ),
        name="decompress",
    )(a, summed, w, new_q)
    return (update, error[None])


def solution(mesh):
    placed = (P("dp", "mp", None), P())
    return jax.shard_map(
        on_device,
        mesh=mesh,
        in_specs=placed,
        out_specs=(P("mp", None), P("dp", "mp", None)),
        check_vma=False,
    )
```

time: 309 us -> 117 us (0.38)
  waiting for transfers between devices: 211 us -> 0 us
  Pallas kernels: 0 us -> 116 us
  other arithmetic: 44 us -> 0 us
  matrix products: 39 us -> 0 us
  between operations: 13.8 us -> 0.64 us
    psum x3 -> x0, waiting for transfers between devices: 141 us -> none  [the longest x1 52.2 us: on_device(): gram = lax.psum(gram, 'mp')]
    pallas_call x0 -> x2, Pallas kernels: none -> 116 us  [the longest x1 92.8 us: on_device(): pl.pallas_call(functools.partial(factors_kernel, n, bits, count), out_sha...]
    reduce_scatter x1 -> x0, waiting for transfers between devices: 40.6 us -> none  [on_device(): lax.psum_scatter(lax.dot_general(corrected, ortho_bf, (((0,), (0,)), ((),...]
    dot_general x4 -> x0, matrix products: 36.9 us -> none  [the longest x1 13.9 us: on_device(): lax.dot_general(ortho_bf, new_q.astype(jnp.bfloat16), (((1,), (1,)), ((),...]
    all_gather x1 -> x0, waiting for transfers between devices: 29.4 us -> none  [on_device(): total_q = lax.all_gather(share, 'mp', axis=0, tiled=True)]
    another operation x5 -> x0, other arithmetic: 22.9 us -> none  [the longest x3 12.4 us: on_device(): chol_lower = jnp.linalg.cholesky(gram)]
    broadcast_in_dim x1 -> x0, other arithmetic: 20.3 us -> none  [on_device(): return (update, new_error[None])]
  transfers between devices with their start and end apart: 5 -> 0, of which waited for: 5 -> 0; matrix products, arithmetic and copies ran while one was open for 0% -> 0% of each run, Pallas kernels for 0% -> 0%
where the time goes in v2:
time: 117 us
  Pallas kernels  116 us (99%)
    pallas_call x1, Pallas kernels, on_device(): pl.pallas_call(functools.partial(factors_kernel, n, bits, count), out_sha...  92.8 us
    pallas_call x1, Pallas kernels, on_device(): pl.pallas_call(functools.partial(last_kernel, n), grid=(count, split), ou...  23 us

profile of v2, /device:TPU:0, one launch (start us, length us, event | category | flops | bytes accessed | tf_op | source)
XLA Modules:
  0.0 116.5 jit_solution(3394886169165096680)
XLA Ops:
  0.6 92.8 %factors.1 = (f32[7,128,256]{2,1,0:T(8,128)}, bf16[4096,128]{1,0:T(8,128)(2,1)}, f32[128,128]{1,0:T(8,128)}) custom-call(bf16[1792,4096]{1,0:T(8,128)(2,1)} %bitcast.2, f32[4096,128]{1,0:T(8,128)} %q_ref.1), custom_call_target="tpu_custom_call" | custom-call | tf_op jit(solution)/shard_map/factors/pallas_call | solution.py:400
  93.5 23.0 %decompress.1 = (f32[1792,4096]{1,0:T(8,128)}, bf16[1792,4096]{1,0:T(8,128)(2,1)}) custom-call(bf16[1792,4096]{1,0:T(8,128)(2,1)} %bitcast.3, f32[7,128,256]{2,1,0:T(8,128)} %get-tuple-element.7.s_ref, f32[128,128]{1,0:T(8,128)} %get-tuple-element.8.w_ref, bf16[4096,128]{1,0:T(8,128)(2,1)} %get-tuple-element.9.nq_ref), custom_call_target="tpu_custom_call" | custom-call | tf_op jit(solution)/shard_map/decompress/pallas_call | solution.py:433

commit v3 on v2

--- a/solution.py
+++ b/solution.py
@@ -10,6 +10,7 @@
 MESH = pl.DeviceIdType.MESH
 HIGHEST = lax.Precision.HIGHEST
 GROUPS = 2
+BLOCK = 256
 VMEM_BYTES = 60 * 1024 * 1024
 
 
@@ -47,7 +48,7 @@
     return inner, outer, edge, mid
 
 
-def factors_kernel(n, bits, count, a_hbm, q_ref, s_ref, nq_ref, w_ref, a_v, own, part, cross, acc, z, got,
+def factors_kernel(n, bits, count, a_hbm, q_ref, ortho_ref, nq_ref, a_v, tot, own, part, cross, acc, z, got,
                    full, gwork, ggot, m_ref, zpart, zcross, a_sem, in_send, out_send, part_recv, cross_recv,
                    tot_recv, rs_send, rs_recv, ag_send, ag_recv, g_send, g_recv, zin_send, zout_send,
                    zpart_recv, zcross_recv, ztot_recv):
@@ -59,7 +60,6 @@
     d = lax.axis_index("dp")
     me = lax.axis_index("mp")
     inner, outer, edge, mid = line_of(n, d)
-    tot = s_ref
 
     def bit(b):
         return lax.rem(me // (1 << b), 2)
@@ -72,7 +72,7 @@
         return pltpu.make_async_copy(a_hbm.at[some], a_v.at[some], a_sem.at[c])
 
     def piece(ref, g, c):
-        return ref.at[c, g * rg:(g + 1) * rg]
+        return ref.at[c, pl.ds(pl.multiple_of(g * rg, rg), rg)]
 
     def send_part(g, c):
         return copy_to("dp", inner, piece(own, g, c), piece(part, g, c), in_send.at[g, c], part_recv.at[g, c])
@@ -120,19 +120,21 @@
         for c in range(count):
             inward(send_cross(1, c), send_part(1, c))
 
-    lag = 1
-
-    def exchange(g, t, carry):
-        @pl.when(jnp.logical_not(edge) & (t < count))
-        def _():
-            send_part(g, t).wait_recv()
-            mine = piece(own, g, t)
-            mine[...] = mine[...] + piece(part, g, t)[...]
-            inward(send_cross(g, t), send_part(g, t))
+    lag = 2
+    total = GROUPS * count
+
+    def exchange(t, carry):
+        @pl.when(jnp.logical_not(edge) & (t < total))
+        def _():
+            g, c = t // count, lax.rem(t, count)
+            send_part(g, c).wait_recv()
+            mine = piece(own, g, c)
+            mine[...] = mine[...] + piece(part, g, c)[...]
+            inward(send_cross(g, c), send_part(g, c))
 
         @pl.when(t >= lag)
         def _():
-            c = t - lag
+            g, c = (t - lag) // count, lax.rem(t - lag, count)
 
             @pl.when(mid)
             def _():
@@ -157,7 +159,9 @@
                 acc[g, :, col:col + step] += jnp.dot(
                     both, a_v[some, col:col + step], preferred_element_type=jnp.float32
                 )
-            if g == GROUPS - 1:
+
+            @pl.when(g == GROUPS - 1)
+            def _():
                 whole = tot[c] / n
                 gwork[0] += lax.dot_general(
                     whole, whole, (((1,), (1,)), ((), ())), precision=HIGHEST,
@@ -166,8 +170,8 @@
 
         return carry
 
-    def run(g, first, last):
-        lax.fori_loop(first, last, functools.partial(exchange, g), 0)
+    def run(first, last):
+        lax.fori_loop(first, last, exchange, 0)
 
     def build(g):
         for block in range(blocks):
@@ -266,14 +270,13 @@
             ag(g, s, j).wait()
 
     acc[...] = jnp.zeros_like(acc)
-    run(0, 0, count + lag)
+    run(0, count + lag)
     build(0)
     rs_start(0, 0)
-    steps = count + lag
-    at = 0
+    at = count + lag
     for j in range(bits):
-        upto = steps * (j + 1) // bits
-        run(1, at, upto)
+        upto = count + lag + count * (j + 1) // bits
+        run(at, upto)
         at = upto
         if j < bits - 1:
             rs_finish(0, j)
@@ -321,7 +324,14 @@
     lane = lax.broadcasted_iota(jnp.int32, (rank, rank), 1)
     pivots = jnp.sum(jnp.where(row == lane, m, 0.0), axis=1, keepdims=True)
     w = jnp.where(lane < row, m, jnp.where(lane == row, 1.0, 0.0)) / jnp.sqrt(pivots)
-    w_ref[...] = w
+
+    def straighten(c, carry):
+        ortho_ref[pl.ds(pl.multiple_of(c * rb, rb), rb), :] = jnp.dot(
+            w, tot[c] / n, precision=HIGHEST, preferred_element_type=jnp.float32
+        ).T.astype(jnp.bfloat16)
+        return carry
+
+    lax.fori_loop(0, count, straighten, 0)
     ag_finish(1, 0)
 
     def turn(block, carry):
@@ -368,11 +378,9 @@
     lax.fori_loop(first, last, pivot, 0)
 
 
-def last_kernel(n, a_ref, s_ref, w_ref, nq_ref, update_ref, error_ref):
-    rank = w_ref.shape[0]
-    ortho = jnp.dot(
-        w_ref[...], s_ref[0] / n, precision=HIGHEST, preferred_element_type=jnp.float32
-    ).T.astype(jnp.bfloat16)
+def last_kernel(a_ref, ortho_ref, nq_ref, update_ref, error_ref):
+    rank = ortho_ref.shape[1]
+    ortho = ortho_ref[...]
     group = 4
     for first in range(0, nq_ref.shape[0] // rank, group):
         right = jnp.concatenate(
@@ -397,17 +405,17 @@
     vmem = pl.BlockSpec(memory_space=pltpu.VMEM)
     dma = pltpu.SemaphoreType.DMA
     flat = wide // GROUPS
-    summed, new_q, w = pl.pallas_call(
+    ortho, new_q = pl.pallas_call(
         functools.partial(factors_kernel, n, bits, count),
         out_shape=(
-            jax.ShapeDtypeStruct((count, rank, rb), f32),
+            jax.ShapeDtypeStruct((rows, rank), bf16),
             jax.ShapeDtypeStruct((wide, rank), bf16),
-            jax.ShapeDtypeStruct((rank, rank), f32),
         ),
         in_specs=[pl.BlockSpec(memory_space=pl.ANY), vmem],
-        out_specs=(vmem, vmem, vmem),
+        out_specs=(vmem, vmem),
         scratch_shapes=[
             pltpu.VMEM((rows, wide), bf16),
+            pltpu.VMEM((count, rank, rb), f32),
             pltpu.VMEM((count, rank, rb), f32),
             pltpu.VMEM((count, rank, rb), f32),
             pltpu.VMEM((count, rank, rb), f32),
@@ -428,27 +436,25 @@
         ),
         name="factors",
     )(a, start_q)
-    split = 2 if rb % 256 == 0 else 1
-    small = rb // split
+    small = BLOCK if rows % BLOCK == 0 else rb
     update, error = pl.pallas_call(
-        functools.partial(last_kernel, n),
-        grid=(count, split),
+        last_kernel,
+        grid=(rows // small,),
         out_shape=(
             jax.ShapeDtypeStruct((rows, wide), f32),
             jax.ShapeDtypeStruct((rows, wide), bf16),
         ),
         in_specs=[
-            pl.BlockSpec((small, wide), lambda i, j: (i * split + j, 0)),
-            pl.BlockSpec((1, rank, small), lambda i, j: (i, 0, j)),
-            pl.BlockSpec((rank, rank), lambda i, j: (0, 0)),
-            pl.BlockSpec((wide, rank), lambda i, j: (0, 0)),
+            pl.BlockSpec((small, wide), lambda i: (i, 0)),
+            pl.BlockSpec((small, rank), lambda i: (i, 0)),
+            pl.BlockSpec((wide, rank), lambda i: (0, 0)),
         ],
         out_specs=(
-            pl.BlockSpec((small, wide), lambda i, j: (i * split + j, 0)),
-            pl.BlockSpec((small, wide), lambda i, j: (i * split + j, 0)),
+            pl.BlockSpec((small, wide), lambda i: (i, 0)),
+            pl.BlockSpec((small, wide), lambda i: (i, 0)),
         ),
         name="decompress",
-    )(a, summed, w, new_q)
+    )(a, ortho, new_q)
     return (update, error[None])
 
 

time: 117 us -> 108 us (0.923)
  Pallas kernels: 116 us -> 107 us
    pallas_call x1, Pallas kernels: 92.8 us -> 86.8 us  [on_device(): pl.pallas_call(functools.partial(factors_kernel, n, bits, count), out_sha...]
    pallas_call x1, Pallas kernels: 23 us -> 20 us  [on_device(): pl.pallas_call(last_kernel, grid=(rows // small,), out_shape=(jax.ShapeDt...]
where the time goes in v3:
time: 108 us; the launch traced here: 107 us
  Pallas kernels  107 us (99%)
    pallas_call x1, Pallas kernels, on_device(): pl.pallas_call(functools.partial(factors_kernel, n, bits, count), out_sha...  86.8 us
    pallas_call x1, Pallas kernels, on_device(): pl.pallas_call(last_kernel, grid=(rows // small,), out_shape=(jax.ShapeDt...  20 us

profile of v3, /device:TPU:0, one launch (start us, length us, event | category | flops | bytes accessed | tf_op | source)
XLA Modules:
  0.0 107.4 jit_solution(16892037108989925987)
XLA Ops:
  0.6 86.8 %factors.1 = (bf16[1792,128]{1,0:T(8,128)(2,1)}, bf16[4096,128]{1,0:T(8,128)(2,1)}) custom-call(bf16[1792,4096]{1,0:T(8,128)(2,1)} %bitcast.2, f32[4096,128]{1,0:T(8,128)} %q_ref.1), custom_call_target="tpu_custom_call" | custom-call | tf_op jit(solution)/shard_map/factors/pallas_call | solution.py:408
  87.4 20.0 %decompress.1 = (f32[1792,4096]{1,0:T(8,128)}, bf16[1792,4096]{1,0:T(8,128)(2,1)}) custom-call(bf16[1792,4096]{1,0:T(8,128)(2,1)} %bitcast.3, bf16[1792,128]{1,0:T(8,128)(2,1)} %get-tuple-element.6.ortho_ref, bf16[4096,128]{1,0:T(8,128)(2,1)} %get-tuple-element.7.nq_ref), custom_call_target="tpu_custom_call" | custom-call | tf_op jit(solution)/shard_map/decompress/pallas_call | solution.py:440
